TPU v7x, 32 devices: a whole 2x2x4 slice. The times are simulated.
32 devices in a mesh: tm: 8 (over z, x), gx: 4 (over y, core).
Axes of the slice: x: 2, y: 2, z: 4, core: 2. Of those that a mesh axis runs over, the one named last changes fastest.
Arguments:
- initial: float32 [8, 256, 256], P('gx'), may hold values from -1 to 1
- node_values: float32 [8, 3, 8, 256, 256], P('tm', None, 'gx'), may hold values from -1 to 1
Outputs:
- solution: float32 [8, 3, 8, 256, 256], P('tm', None, 'gx')
All inputs are finite; a program needn't handle non-finite values.
Results may differ from a plain program's by a relative error of at most 0.0002.
Values sent between devices are 32-bit elements; how exact they have to be, the bound alone decides.
No kernel may reach another device: no remote copies, remote signals or barrier semaphores. Data moves between devices by JAX's collectives and lax.ppermute only.
A program may use at most 64 MiB of HBM per device.

v0:
```python
import math

import jax
import jax.numpy as jnp
import numpy as np
from jax import lax
from jax.experimental import pallas as pl
from jax.experimental.pallas import tpu as pltpu
from jax.sharding import PartitionSpec as P


SWEEPS = 2
SHARES = (9, 11, 12)
RING = ("100", "110")

spacing = 2.0
step_size = 0.2
half_step = 0.1

MIDDLE = (
    step_size * 5.0 / 24.0 - half_step,
    step_size / 3.0,
    -step_size / 24.0,
)
FINAL = (
    -step_size / 24.0,
    step_size / 3.0 - half_step,
    step_size * 5.0 / 24.0,
)


def second_derivative(count):
    offset = np.arange(count)[None, :] - np.arange(count)[:, None]
    angle_step = 2.0 * math.pi / count
    sine = np.sin(np.where(offset == 0, 1, offset) * (angle_step / 2.0))
    off_value = -0.5 * np.where(offset % 2 == 0, 1.0, -1.0) / (sine * sine)
    diagonal = -(math.pi**2) / (3.0 * angle_step * angle_step) - 1.0 / 6.0
    matrix = np.where(offset == 0, diagonal, off_value) * (angle_step / spacing) ** 2
    return matrix.astype(np.float32)


def relayed(shard, name):
    length = lax.axis_size("tm")
    if RING[int(name[6])][int(name[8])] == "1":
        return lax.ppermute(shard, "tm", [(i, (i + 1) % length) for i in range(length)])
    return lax.ppermute(shard, "tm", [(i, i + 1) for i in range(length - 1)])


def neighbours(part):
    count = lax.axis_size("gx")
    head, tail = part[:2], part[part.shape[0] - 2 :]
    if count % 2:
        left = lax.ppermute(tail, "gx", [(i, (i + 1) % count) for i in range(count)])
        right = lax.ppermute(head, "gx", [((i + 1) % count, i) for i in range(count)])
        return (left, left), (right, right)
    even = lax.axis_index("gx") % 2 == 0
    inner, outer = [], []
    for i in range(0, count, 2):
        inner += [(i, i + 1), (i + 1, i)]
        outer += [(i + 1, (i + 2) % count), ((i + 2) % count, i + 1)]
    if part.shape[0] == 2:
        to_inner = to_outer = part
    else:
        to_inner = jnp.where(even, tail, head)
        to_outer = jnp.where(even, head, tail)
    across = lax.ppermute(to_outer, "gx", outer)
    beside = lax.ppermute(to_inner, "gx", inner)
    return (across, beside), (beside, across)


def stencil(part, left, right):
    planes = [left[0], left[1], *part, right[0], right[1]]
    rows = []
    for i in range(2, len(planes) - 2):
        near = planes[i - 1] + planes[i + 1]
        far = planes[i - 2] + planes[i + 2]
        rows.append((16.0 * near - far - 18.0 * planes[i]) * (1.0 / 12.0))
    return jnp.stack(rows)


def halves(matrix):
    high = matrix.astype(jnp.bfloat16)
    return high, (matrix - high.astype(np.float32)).astype(jnp.bfloat16)


def products(parts, halves_y, halves_z):
    slabs, _, columns = parts[0].shape
    tops = [0]
    for part in parts:
        tops.append(tops[-1] + part.shape[1])

    def body(*refs):
        pieces = refs[: len(parts)]
        y_high, y_low, z_high, z_low, out = refs[len(parts) : len(parts) + 5]
        dot = lambda a, b: jnp.dot(a, b, preferred_element_type=jnp.float32)
        for slab in range(slabs):
            field = jnp.concatenate([piece[slab] for piece in pieces], axis=0)
            high, low = halves(field)
            term = dot(y_high[...], high) + (dot(y_high[...], low) + dot(y_low[...], high))
            term += dot(high, z_high[...]) + (dot(low, z_high[...]) + dot(high, z_low[...]))
            out[slab] = term

    rows = tops[-1]
    vmem = pl.BlockSpec(memory_space=pltpu.VMEM)
    return pl.pallas_call(
        body,
        out_shape=jax.ShapeDtypeStruct((slabs, rows, columns), jnp.float32),
        in_specs=[vmem] * (len(parts) + 4),
        out_specs=vmem,
        compiler_params=pltpu.CompilerParams(vmem_limit_bytes=16 * 1024 * 1024),
        cost_estimate=pl.CostEstimate(
            flops=6 * 2 * slabs * rows * columns * (rows + columns) // 2,
            bytes_accessed=8 * slabs * rows * columns,
            transcendentals=0,
        ),
    )(*parts, *halves_y, *halves_z)


def weighted(weights, parts):
    return sum(w * p for w, p in zip(weights, parts))


def sweeps(initial, node_values):
    rows = node_values.shape[3]
    matrix_y = halves(second_derivative(rows))
    matrix_z = halves(second_derivative(node_values.shape[4]))
    leading = lax.axis_index("tm") == 0
    parts = range(len(SHARES))
    cuts = [rows * sum(SHARES[: i + 1]) // sum(SHARES) for i in parts][:-1]
    cut = lambda item: jnp.split(item, cuts, axis=1)
    join = lambda items: jnp.concatenate(items, axis=1)
    start = cut(initial)
    values = [cut(node_values[0, m]) for m in range(3)]
    for sweep in range(SWEEPS):
        old = list(zip(*values))
        linear_one = [weighted(MIDDLE, u) for u in old]
        linear_two = [weighted(FINAL, u) for u in old]
        cubic_one = [weighted(MIDDLE, [x * x * x for x in u]) for u in old]
        cubic_two = [weighted(FINAL, [x * x * x for x in u]) for u in old]
        arrived = [relayed(old[i][2], f"relay_{sweep}_{i}") for i in parts]
        first, drive = [], []
        for i in parts:
            first.append(jnp.where(leading, start[i], arrived[i]))
            drive.append(half_step * first[i] + linear_one[i])
        halos = [neighbours(drive[i]) for i in parts]
        whole = products(drive, matrix_y, matrix_z)
        terms = cut(whole)
        middle, drive_two = [], []
        for i in parts:
            middle.append(update(first[i], cubic_one[i], terms[i], drive[i], halos[i]))
            drive_two.append(half_step * middle[i] + linear_two[i])
        halos = [neighbours(drive_two[i]) for i in parts]
        whole = products(drive_two, matrix_y, matrix_z)
        terms = cut(whole)
        if sweep + 1 == SWEEPS:
            out = jnp.stack([join(v) for v in (first, middle, middle)])[None]
        final = []
        for i in parts:
            final.append(update(middle[i], cubic_two[i], terms[i], drive_two[i], halos[i]))
            if sweep + 1 == SWEEPS:
                row = ([0] + cuts)[i]
                out = lax.dynamic_update_slice(out, final[i][None, None], (0, 2, 0, row, 0))
        values = [first, middle, final]
    return out


def update(known, cubic, term, drive, halo):
    base = known - half_step * known * known * known - cubic
    halo = [jnp.where(lax.axis_index("gx") % 2 == 0, *pair) for pair in halo]
    return base + (term + stencil(drive, *halo))


def solution(mesh):
    in_specs = (P("gx", None, None), P("tm", None, "gx", None, None))
    out_specs = P("tm", None, "gx", None, None)
    return jax.shard_map(sweeps, mesh=mesh, in_specs=in_specs, out_specs=out_specs, check_vma=False)
```

profile of v0, /device:TPU:29, one launch (start us, length us, event | category | flops | bytes accessed | tf_op | source)
XLA Modules:
  0.0 66.9 jit_solution(16107949430518224026)
XLA Ops:
  0.0 1.5 %slice_bitcast_fusion.2 = (f32[2,256,256]{2,1,0:T(8,128)S(1)}, f32[2,256,256]{2,1,0:T(8,128)S(1)}, f32[2,256,256]{2,1,0:T(8,128)S(1)}) fusion(f32[1,3,2,256,256]{4,3,2,1,0:T(8,128)} %param.7), kind=kLoop, calls=%fused_computation.5 | loop fusion | bytes 3145728 | tf_op jit(solution)/shard_map/squeeze | solution.py:133
  1.5 1.3 %collective-permute-start = (f32[2,72,256]{2,1,0:T(8,128)S(1)}, f32[2,72,256]{2,1,0:T(8,128)S(1)}, u32[]{:S(2)}, u32[]{:S(2)}) collective-permute-start(f32[2,72,256]{2,1,0:T(8,128)S(1)} %split.96), channel_id=1, source_target_pairs={{0,4},{4,8},{8,12},{12,16},{16,20},{20,24},{24,28},{28,0},{1,5},{5... | collective-permute-start | bytes 442376 | tf_op jit(solution)/shard_map/ppermute | solution.py:45
  2.8 1.9 %collective-permute-start.1 = (f32[2,88,256]{2,1,0:T(8,128)S(1)}, f32[2,88,256]{2,1,0:T(8,128)S(1)}, u32[]{:S(2)}, u32[]{:S(2)}) collective-permute-start(f32[2,88,256]{2,1,0:T(8,128)S(1)} %split.99), channel_id=1, source_target_pairs={{0,4},{4,8},{8,12},{12,16},{16,20},{20,24},{24,28},{1,5},{5,9},{9,... | collective-permute-start | bytes 540680 | tf_op jit(solution)/shard_map/ppermute | solution.py:46
  4.8 1.9 %collective-permute-start.2 = (f32[2,96,256]{2,1,0:T(8,128)S(1)}, f32[2,96,256]{2,1,0:T(8,128)S(1)}, u32[]{:S(2)}, u32[]{:S(2)}) collective-permute-start(f32[2,96,256]{2,1,0:T(8,128)S(1)} %split.102), channel_id=1, source_target_pairs={{0,4},{4,8},{8,12},{12,16},{16,20},{20,24},{24,28},{1,5},{5,9},{9,... | collective-permute-start | bytes 589832 | tf_op jit(solution)/shard_map/ppermute | solution.py:46
  7.3 1.6 %collective-permute-start.4 = (f32[2,72,256]{2,1,0:T(8,128)S(1)}, f32[2,72,256]{2,1,0:T(8,128)S(1)}, u32[]{:S(2)}, u32[]{:S(2)}) collective-permute-start(f32[2,72,256]{2,1,0:T(8,128)S(1)} %get-tuple-element.27.refs_0_), channel_id=1, source_target_pairs={{0,1},{1,0},{2,3},{3,2},{4,5},{5,4},{6,7},{7,6},{8,9},{9,8},{10,11... | collective-permute-start | bytes 442376 | tf_op jit(solution)/shard_map/ppermute | solution.py:67
  9.1 1.7 %collective-permute-done.1 = f32[2,88,256]{2,1,0:T(8,128)S(1)} collective-permute-done((f32[2,88,256]{2,1,0:T(8,128)S(1)}, f32[2,88,256]{2,1,0:T(8,128)S(1)}, u32[]{:S(2)}, u32[]{:S(2)}) %collective-permute-start.1) | collective-permute-done | bytes 180256 | tf_op jit(solution)/shard_map/ppermute | solution.py:46
  10.9 3.2 %collective-permute-start.6 = (f32[2,88,256]{2,1,0:T(8,128)S(1)}, f32[2,88,256]{2,1,0:T(8,128)S(1)}, u32[]{:S(2)}, u32[]{:S(2)}) collective-permute-start(f32[2,88,256]{2,1,0:T(8,128)S(1)} %get-tuple-element.25.refs_1_), channel_id=1, source_target_pairs={{0,1},{1,0},{2,3},{3,2},{4,5},{5,4},{6,7},{7,6},{8,9},{9,8},{10,11... | collective-permute-start | bytes 540680 | tf_op jit(solution)/shard_map/ppermute | solution.py:67
  15.1 1.8 %collective-permute-start.8 = (f32[2,96,256]{2,1,0:T(8,128)S(1)}, f32[2,96,256]{2,1,0:T(8,128)S(1)}, u32[]{:S(2)}, u32[]{:S(2)}) collective-permute-start(f32[2,96,256]{2,1,0:T(8,128)S(1)} %get-tuple-element.23.refs_2_), channel_id=1, source_target_pairs={{0,1},{1,0},{2,3},{3,2},{4,5},{5,4},{6,7},{7,6},{8,9},{9,8},{10,11... | collective-permute-start | bytes 589832 | tf_op jit(solution)/shard_map/ppermute | solution.py:67
  18.6 1.2 %collective-permute-start.9 = (f32[2,72,256]{2,1,0:T(8,128)S(1)}, f32[2,72,256]{2,1,0:T(8,128)S(1)}, u32[]{:S(2)}, u32[]{:S(2)}) collective-permute-start(f32[2,72,256]{2,1,0:T(8,128)S(1)} %get-tuple-element.21.refs_0_), channel_id=1, source_target_pairs={{1,2},{2,1},{3,0},{0,3},{5,6},{6,5},{7,4},{4,7},{9,10},{10,9},{11,... | collective-permute-start | bytes 442376 | tf_op jit(solution)/shard_map/ppermute | solution.py:66
  19.8 1.3 %collective-permute-done.5 = f32[2,88,256]{2,1,0:T(8,128)S(1)} collective-permute-done((f32[2,88,256]{2,1,0:T(8,128)S(1)}, f32[2,88,256]{2,1,0:T(8,128)S(1)}, u32[]{:S(2)}, u32[]{:S(2)}) %collective-permute-start.5) | collective-permute-done | bytes 180256 | tf_op jit(solution)/shard_map/ppermute | solution.py:66
  22.0 3.3 %collective-permute-done.7 = f32[2,96,256]{2,1,0:T(8,128)S(1)} collective-permute-done((f32[2,96,256]{2,1,0:T(8,128)S(1)}, f32[2,96,256]{2,1,0:T(8,128)S(1)}, u32[]{:S(2)}, u32[]{:S(2)}) %collective-permute-start.7) | collective-permute-done | bytes 196640 | tf_op jit(solution)/shard_map/ppermute | solution.py:66
  26.9 1.5 %collective-permute-done.9 = f32[2,72,256]{2,1,0:T(8,128)S(1)} collective-permute-done((f32[2,72,256]{2,1,0:T(8,128)S(1)}, f32[2,72,256]{2,1,0:T(8,128)S(1)}, u32[]{:S(2)}, u32[]{:S(2)}) %collective-permute-start.9) | collective-permute-done | bytes 147488 | tf_op jit(solution)/shard_map/ppermute | solution.py:66
  28.9 3.4 %collective-permute-done.12 = f32[2,88,256]{2,1,0:T(8,128)S(1)} collective-permute-done((f32[2,88,256]{2,1,0:T(8,128)S(1)}, f32[2,88,256]{2,1,0:T(8,128)S(1)}, u32[]{:S(2)}, u32[]{:S(2)}) %collective-permute-start.12) | collective-permute-done | bytes 180256 | tf_op jit(solution)/shard_map/ppermute | solution.py:66
  32.7 2.6 %collective-permute-done.11 = f32[2,72,256]{2,1,0:T(8,128)S(1)} collective-permute-done((f32[2,72,256]{2,1,0:T(8,128)S(1)}, f32[2,72,256]{2,1,0:T(8,128)S(1)}, u32[]{:S(2)}, u32[]{:S(2)}) %collective-permute-start.11) | collective-permute-done | bytes 147488 | tf_op jit(solution)/shard_map/ppermute | solution.py:45
  36.4 1.9 %collective-permute-start.17 = (f32[2,96,256]{2,1,0:T(8,128)S(1)}, f32[2,96,256]{2,1,0:T(8,128)S(1)}, u32[]{:S(2)}, u32[]{:S(2)}) collective-permute-start(f32[2,96,256]{2,1,0:T(8,128)S(1)} %fusion.3), channel_id=1, source_target_pairs={{0,4},{4,8},{8,12},{12,16},{16,20},{20,24},{24,28},{1,5},{5,9},{9,... | collective-permute-start | bytes 589832 | tf_op jit(solution)/shard_map/ppermute | solution.py:46
  38.3 1.6 %collective-permute-done.14 = f32[2,88,256]{2,1,0:T(8,128)S(1)} collective-permute-done((f32[2,88,256]{2,1,0:T(8,128)S(1)}, f32[2,88,256]{2,1,0:T(8,128)S(1)}, u32[]{:S(2)}, u32[]{:S(2)}) %collective-permute-start.14) | collective-permute-done | bytes 180256 | tf_op jit(solution)/shard_map/ppermute | solution.py:45
  41.6 3.6 %collective-permute-done.17 = f32[2,96,256]{2,1,0:T(8,128)S(1)} collective-permute-done((f32[2,96,256]{2,1,0:T(8,128)S(1)}, f32[2,96,256]{2,1,0:T(8,128)S(1)}, u32[]{:S(2)}, u32[]{:S(2)}) %collective-permute-start.17) | collective-permute-done | bytes 196640 | tf_op jit(solution)/shard_map/ppermute | solution.py:46
  46.0 1.4 %collective-permute-start.25 = (f32[2,72,256]{2,1,0:T(8,128)S(1)}, f32[2,72,256]{2,1,0:T(8,128)S(1)}, u32[]{:S(2)}, u32[]{:S(2)}) collective-permute-start(f32[2,72,256]{2,1,0:T(8,128)S(1)} %get-tuple-element.9.refs_0_), channel_id=1, source_target_pairs={{0,1},{1,0},{2,3},{3,2},{4,5},{5,4},{6,7},{7,6},{8,9},{9,8},{10,11... | collective-permute-start | bytes 442376 | tf_op jit(solution)/shard_map/ppermute | solution.py:67
  47.4 1.2 %collective-permute-start.24 = (f32[2,72,256]{2,1,0:T(8,128)S(1)}, f32[2,72,256]{2,1,0:T(8,128)S(1)}, u32[]{:S(2)}, u32[]{:S(2)}) collective-permute-start(f32[2,72,256]{2,1,0:T(8,128)S(1)} %get-tuple-element.9.refs_0_), channel_id=1, source_target_pairs={{1,2},{2,1},{3,0},{0,3},{5,6},{6,5},{7,4},{4,7},{9,10},{10,9},{11,... | collective-permute-start | bytes 442376 | tf_op jit(solution)/shard_map/ppermute | solution.py:66
  50.1 1.2 %collective-permute-start.26 = (f32[2,88,256]{2,1,0:T(8,128)S(1)}, f32[2,88,256]{2,1,0:T(8,128)S(1)}, u32[]{:S(2)}, u32[]{:S(2)}) collective-permute-start(f32[2,88,256]{2,1,0:T(8,128)S(1)} %get-tuple-element.7.refs_1_), channel_id=1, source_target_pairs={{1,2},{2,1},{3,0},{0,3},{5,6},{6,5},{7,4},{4,7},{9,10},{10,9},{11,... | collective-permute-start | bytes 540680 | tf_op jit(solution)/shard_map/ppermute | solution.py:66
  51.3 2.5 %collective-permute-done.24 = f32[2,72,256]{2,1,0:T(8,128)S(1)} collective-permute-done((f32[2,72,256]{2,1,0:T(8,128)S(1)}, f32[2,72,256]{2,1,0:T(8,128)S(1)}, u32[]{:S(2)}, u32[]{:S(2)}) %collective-permute-start.24) | collective-permute-done | bytes 147488 | tf_op jit(solution)/shard_map/ppermute | solution.py:66
  53.9 4.1 %collective-permute-done.22 = f32[2,96,256]{2,1,0:T(8,128)S(1)} collective-permute-done((f32[2,96,256]{2,1,0:T(8,128)S(1)}, f32[2,96,256]{2,1,0:T(8,128)S(1)}, u32[]{:S(2)}, u32[]{:S(2)}) %collective-permute-start.22) | collective-permute-done | bytes 196640 | tf_op jit(solution)/shard_map/ppermute | solution.py:66
  59.0 1.6 %collective-permute-start.28 = (f32[2,96,256]{2,1,0:T(8,128)S(1)}, f32[2,96,256]{2,1,0:T(8,128)S(1)}, u32[]{:S(2)}, u32[]{:S(2)}) collective-permute-start(f32[2,96,256]{2,1,0:T(8,128)S(1)} %get-tuple-element.5.refs_2_), channel_id=1, source_target_pairs={{1,2},{2,1},{3,0},{0,3},{5,6},{6,5},{7,4},{4,7},{9,10},{10,9},{11,... | collective-permute-start | bytes 589832 | tf_op jit(solution)/shard_map/ppermute | solution.py:66
  61.2 4.8 %collective-permute-done.28 = f32[2,96,256]{2,1,0:T(8,128)S(1)} collective-permute-done((f32[2,96,256]{2,1,0:T(8,128)S(1)}, f32[2,96,256]{2,1,0:T(8,128)S(1)}, u32[]{:S(2)}, u32[]{:S(2)}) %collective-permute-start.28) | collective-permute-done | bytes 196640 | tf_op jit(solution)/shard_map/ppermute | solution.py:66
  (97 shorter events, 14.0 us)
Async XLA Ops:
  2.8 8.0 %collective-permute-start.1 = (f32[2,88,256]{2,1,0:T(8,128)S(1)}, f32[2,88,256]{2,1,0:T(8,128)S(1)}, u32[]{:S(2)}, u32[]{:S(2)}) collective-permute-start(f32[2,88,256]{2,1,0:T(8,128)S(1)} %split.99), channel_id=1, source_target_pairs={{0,4},{4,8},{8,12},{12,16},{16,20},{20,24},{24,28},{1,5},{5,9},{9,... | collective-permute-start | bytes 540680 | tf_op jit(solution)/shard_map/ppermute | solution.py:46
  4.8 10.3 %collective-permute-start.2 = (f32[2,96,256]{2,1,0:T(8,128)S(1)}, f32[2,96,256]{2,1,0:T(8,128)S(1)}, u32[]{:S(2)}, u32[]{:S(2)}) collective-permute-start(f32[2,96,256]{2,1,0:T(8,128)S(1)} %split.102), channel_id=1, source_target_pairs={{0,4},{4,8},{8,12},{12,16},{16,20},{20,24},{24,28},{1,5},{5,9},{9,... | collective-permute-start | bytes 589832 | tf_op jit(solution)/shard_map/ppermute | solution.py:46
  7.3 10.3 %collective-permute-start.4 = (f32[2,72,256]{2,1,0:T(8,128)S(1)}, f32[2,72,256]{2,1,0:T(8,128)S(1)}, u32[]{:S(2)}, u32[]{:S(2)}) collective-permute-start(f32[2,72,256]{2,1,0:T(8,128)S(1)} %get-tuple-element.27.refs_0_), channel_id=1, source_target_pairs={{0,1},{1,0},{2,3},{3,2},{4,5},{5,4},{6,7},{7,6},{8,9},{9,8},{10,11... | collective-permute-start | bytes 442376 | tf_op jit(solution)/shard_map/ppermute | solution.py:67
  9.0 8.8 %collective-permute-start.3 = (f32[2,72,256]{2,1,0:T(8,128)S(1)}, f32[2,72,256]{2,1,0:T(8,128)S(1)}, u32[]{:S(2)}, u32[]{:S(2)}) collective-permute-start(f32[2,72,256]{2,1,0:T(8,128)S(1)} %get-tuple-element.27.refs_0_), channel_id=1, source_target_pairs={{1,2},{2,1},{3,0},{0,3},{5,6},{6,5},{7,4},{4,7},{9,10},{10,9},{11,... | collective-permute-start | bytes 442376 | tf_op jit(solution)/shard_map/ppermute | solution.py:66
  10.9 7.6 %collective-permute-start.6 = (f32[2,88,256]{2,1,0:T(8,128)S(1)}, f32[2,88,256]{2,1,0:T(8,128)S(1)}, u32[]{:S(2)}, u32[]{:S(2)}) collective-permute-start(f32[2,88,256]{2,1,0:T(8,128)S(1)} %get-tuple-element.25.refs_1_), channel_id=1, source_target_pairs={{0,1},{1,0},{2,3},{3,2},{4,5},{5,4},{6,7},{7,6},{8,9},{9,8},{10,11... | collective-permute-start | bytes 540680 | tf_op jit(solution)/shard_map/ppermute | solution.py:67
  14.1 6.9 %collective-permute-start.5 = (f32[2,88,256]{2,1,0:T(8,128)S(1)}, f32[2,88,256]{2,1,0:T(8,128)S(1)}, u32[]{:S(2)}, u32[]{:S(2)}) collective-permute-start(f32[2,88,256]{2,1,0:T(8,128)S(1)} %get-tuple-element.25.refs_1_), channel_id=1, source_target_pairs={{1,2},{2,1},{3,0},{0,3},{5,6},{6,5},{7,4},{4,7},{9,10},{10,9},{11,... | collective-permute-start | bytes 540680 | tf_op jit(solution)/shard_map/ppermute | solution.py:66
  15.1 6.2 %collective-permute-start.8 = (f32[2,96,256]{2,1,0:T(8,128)S(1)}, f32[2,96,256]{2,1,0:T(8,128)S(1)}, u32[]{:S(2)}, u32[]{:S(2)}) collective-permute-start(f32[2,96,256]{2,1,0:T(8,128)S(1)} %get-tuple-element.23.refs_2_), channel_id=1, source_target_pairs={{0,1},{1,0},{2,3},{3,2},{4,5},{5,4},{6,7},{7,6},{8,9},{9,8},{10,11... | collective-permute-start | bytes 589832 | tf_op jit(solution)/shard_map/ppermute | solution.py:67
  17.6 7.7 %collective-permute-start.7 = (f32[2,96,256]{2,1,0:T(8,128)S(1)}, f32[2,96,256]{2,1,0:T(8,128)S(1)}, u32[]{:S(2)}, u32[]{:S(2)}) collective-permute-start(f32[2,96,256]{2,1,0:T(8,128)S(1)} %get-tuple-element.23.refs_2_), channel_id=1, source_target_pairs={{1,2},{2,1},{3,0},{0,3},{5,6},{6,5},{7,4},{4,7},{9,10},{10,9},{11,... | collective-permute-start | bytes 589832 | tf_op jit(solution)/shard_map/ppermute | solution.py:66
  18.0 8.2 %collective-permute-start.10 = (f32[2,72,256]{2,1,0:T(8,128)S(1)}, f32[2,72,256]{2,1,0:T(8,128)S(1)}, u32[]{:S(2)}, u32[]{:S(2)}) collective-permute-start(f32[2,72,256]{2,1,0:T(8,128)S(1)} %get-tuple-element.21.refs_0_), channel_id=1, source_target_pairs={{0,1},{1,0},{2,3},{3,2},{4,5},{5,4},{6,7},{7,6},{8,9},{9,8},{10,11... | collective-permute-start | bytes 442376 | tf_op jit(solution)/shard_map/ppermute | solution.py:67
  18.6 9.9 %collective-permute-start.9 = (f32[2,72,256]{2,1,0:T(8,128)S(1)}, f32[2,72,256]{2,1,0:T(8,128)S(1)}, u32[]{:S(2)}, u32[]{:S(2)}) collective-permute-start(f32[2,72,256]{2,1,0:T(8,128)S(1)} %get-tuple-element.21.refs_0_), channel_id=1, source_target_pairs={{1,2},{2,1},{3,0},{0,3},{5,6},{6,5},{7,4},{4,7},{9,10},{10,9},{11,... | collective-permute-start | bytes 442376 | tf_op jit(solution)/shard_map/ppermute | solution.py:66
  21.3 7.5 %collective-permute-start.13 = (f32[2,88,256]{2,1,0:T(8,128)S(1)}, f32[2,88,256]{2,1,0:T(8,128)S(1)}, u32[]{:S(2)}, u32[]{:S(2)}) collective-permute-start(f32[2,88,256]{2,1,0:T(8,128)S(1)} %get-tuple-element.19.refs_1_), channel_id=1, source_target_pairs={{0,1},{1,0},{2,3},{3,2},{4,5},{5,4},{6,7},{7,6},{8,9},{9,8},{10,11... | collective-permute-start | bytes 540680 | tf_op jit(solution)/shard_map/ppermute | solution.py:67
  21.4 10.9 %collective-permute-start.12 = (f32[2,88,256]{2,1,0:T(8,128)S(1)}, f32[2,88,256]{2,1,0:T(8,128)S(1)}, u32[]{:S(2)}, u32[]{:S(2)}) collective-permute-start(f32[2,88,256]{2,1,0:T(8,128)S(1)} %get-tuple-element.19.refs_1_), channel_id=1, source_target_pairs={{1,2},{2,1},{3,0},{0,3},{5,6},{6,5},{7,4},{4,7},{9,10},{10,9},{11,... | collective-permute-start | bytes 540680 | tf_op jit(solution)/shard_map/ppermute | solution.py:66
  25.5 10.6 %collective-permute-start.16 = (f32[2,96,256]{2,1,0:T(8,128)S(1)}, f32[2,96,256]{2,1,0:T(8,128)S(1)}, u32[]{:S(2)}, u32[]{:S(2)}) collective-permute-start(f32[2,96,256]{2,1,0:T(8,128)S(1)} %get-tuple-element.17.refs_2_), channel_id=1, source_target_pairs={{0,1},{1,0},{2,3},{3,2},{4,5},{5,4},{6,7},{7,6},{8,9},{9,8},{10,11... | collective-permute-start | bytes 589832 | tf_op jit(solution)/shard_map/ppermute | solution.py:67
  26.2 9.9 %collective-permute-start.15 = (f32[2,96,256]{2,1,0:T(8,128)S(1)}, f32[2,96,256]{2,1,0:T(8,128)S(1)}, u32[]{:S(2)}, u32[]{:S(2)}) collective-permute-start(f32[2,96,256]{2,1,0:T(8,128)S(1)} %get-tuple-element.17.refs_2_), channel_id=1, source_target_pairs={{1,2},{2,1},{3,0},{0,3},{5,6},{6,5},{7,4},{4,7},{9,10},{10,9},{11,... | collective-permute-start | bytes 589832 | tf_op jit(solution)/shard_map/ppermute | solution.py:66
  28.6 6.7 %collective-permute-start.11 = (f32[2,72,256]{2,1,0:T(8,128)S(1)}, f32[2,72,256]{2,1,0:T(8,128)S(1)}, u32[]{:S(2)}, u32[]{:S(2)}) collective-permute-start(f32[2,72,256]{2,1,0:T(8,128)S(1)} %fusion.23), channel_id=1, source_target_pairs={{0,4},{4,8},{8,12},{12,16},{16,20},{20,24},{24,28},{28,0},{1,5},{5... | collective-permute-start | bytes 442376 | tf_op jit(solution)/shard_map/ppermute | solution.py:45
  32.5 7.5 %collective-permute-start.14 = (f32[2,88,256]{2,1,0:T(8,128)S(1)}, f32[2,88,256]{2,1,0:T(8,128)S(1)}, u32[]{:S(2)}, u32[]{:S(2)}) collective-permute-start(f32[2,88,256]{2,1,0:T(8,128)S(1)} %fusion.13), channel_id=1, source_target_pairs={{0,4},{4,8},{8,12},{12,16},{16,20},{20,24},{24,28},{28,0},{1,5},{5... | collective-permute-start | bytes 540680 | tf_op jit(solution)/shard_map/ppermute | solution.py:45
  36.4 8.8 %collective-permute-start.17 = (f32[2,96,256]{2,1,0:T(8,128)S(1)}, f32[2,96,256]{2,1,0:T(8,128)S(1)}, u32[]{:S(2)}, u32[]{:S(2)}) collective-permute-start(f32[2,96,256]{2,1,0:T(8,128)S(1)} %fusion.3), channel_id=1, source_target_pairs={{0,4},{4,8},{8,12},{12,16},{16,20},{20,24},{24,28},{1,5},{5,9},{9,... | collective-permute-start | bytes 589832 | tf_op jit(solution)/shard_map/ppermute | solution.py:46
  40.0 9.0 %collective-permute-start.21 = (f32[2,88,256]{2,1,0:T(8,128)S(1)}, f32[2,88,256]{2,1,0:T(8,128)S(1)}, u32[]{:S(2)}, u32[]{:S(2)}) collective-permute-start(f32[2,88,256]{2,1,0:T(8,128)S(1)} %get-tuple-element.13.refs_1_), channel_id=1, source_target_pairs={{0,1},{1,0},{2,3},{3,2},{4,5},{5,4},{6,7},{7,6},{8,9},{9,8},{10,11... | collective-permute-start | bytes 540680 | tf_op jit(solution)/shard_map/ppermute | solution.py:67
  40.6 8.7 %collective-permute-start.20 = (f32[2,88,256]{2,1,0:T(8,128)S(1)}, f32[2,88,256]{2,1,0:T(8,128)S(1)}, u32[]{:S(2)}, u32[]{:S(2)}) collective-permute-start(f32[2,88,256]{2,1,0:T(8,128)S(1)} %get-tuple-element.13.refs_1_), channel_id=1, source_target_pairs={{1,2},{2,1},{3,0},{0,3},{5,6},{6,5},{7,4},{4,7},{9,10},{10,9},{11,... | collective-permute-start | bytes 540680 | tf_op jit(solution)/shard_map/ppermute | solution.py:66
  47.4 6.4 %collective-permute-start.24 = (f32[2,72,256]{2,1,0:T(8,128)S(1)}, f32[2,72,256]{2,1,0:T(8,128)S(1)}, u32[]{:S(2)}, u32[]{:S(2)}) collective-permute-start(f32[2,72,256]{2,1,0:T(8,128)S(1)} %get-tuple-element.9.refs_0_), channel_id=1, source_target_pairs={{1,2},{2,1},{3,0},{0,3},{5,6},{6,5},{7,4},{4,7},{9,10},{10,9},{11,... | collective-permute-start | bytes 442376 | tf_op jit(solution)/shard_map/ppermute | solution.py:66
  49.0 9.0 %collective-permute-start.22 = (f32[2,96,256]{2,1,0:T(8,128)S(1)}, f32[2,96,256]{2,1,0:T(8,128)S(1)}, u32[]{:S(2)}, u32[]{:S(2)}) collective-permute-start(f32[2,96,256]{2,1,0:T(8,128)S(1)} %get-tuple-element.11.refs_2_), channel_id=1, source_target_pairs={{1,2},{2,1},{3,0},{0,3},{5,6},{6,5},{7,4},{4,7},{9,10},{10,9},{11,... | collective-permute-start | bytes 589832 | tf_op jit(solution)/shard_map/ppermute | solution.py:66
  49.6 11.3 %collective-permute-start.27 = (f32[2,88,256]{2,1,0:T(8,128)S(1)}, f32[2,88,256]{2,1,0:T(8,128)S(1)}, u32[]{:S(2)}, u32[]{:S(2)}) collective-permute-start(f32[2,88,256]{2,1,0:T(8,128)S(1)} %get-tuple-element.7.refs_1_), channel_id=1, source_target_pairs={{0,1},{1,0},{2,3},{3,2},{4,5},{5,4},{6,7},{7,6},{8,9},{9,8},{10,11... | collective-permute-start | bytes 540680 | tf_op jit(solution)/shard_map/ppermute | solution.py:67
  50.1 10.9 %collective-permute-start.26 = (f32[2,88,256]{2,1,0:T(8,128)S(1)}, f32[2,88,256]{2,1,0:T(8,128)S(1)}, u32[]{:S(2)}, u32[]{:S(2)}) collective-permute-start(f32[2,88,256]{2,1,0:T(8,128)S(1)} %get-tuple-element.7.refs_1_), channel_id=1, source_target_pairs={{1,2},{2,1},{3,0},{0,3},{5,6},{6,5},{7,4},{4,7},{9,10},{10,9},{11,... | collective-permute-start | bytes 540680 | tf_op jit(solution)/shard_map/ppermute | solution.py:66
  59.0 7.0 %collective-permute-start.28 = (f32[2,96,256]{2,1,0:T(8,128)S(1)}, f32[2,96,256]{2,1,0:T(8,128)S(1)}, u32[]{:S(2)}, u32[]{:S(2)}) collective-permute-start(f32[2,96,256]{2,1,0:T(8,128)S(1)} %get-tuple-element.5.refs_2_), channel_id=1, source_target_pairs={{1,2},{2,1},{3,0},{0,3},{5,6},{6,5},{7,4},{4,7},{9,10},{10,9},{11,... | collective-permute-start | bytes 589832 | tf_op jit(solution)/shard_map/ppermute | solution.py:66
  (10 other events, 59.8 us)
where the time goes:
time: 68.1 us; the launch traced here: 66.9 us
  waiting for transfers between devices  32.7 us (48%)
  starting transfers between devices  26 us (38%)
  other arithmetic  3.75 us (6%)
  Pallas kernels  2.37 us (3%)
  local copies, waits for them, and re-layouts  1.58 us (2%)
    ppermute x12, waiting for transfers between devices, neighbours(): across = lax.ppermute(to_outer, 'gx', outer)  21.8 us
    ppermute x12, starting transfers between devices, neighbours(): beside = lax.ppermute(to_inner, 'gx', inner)  10.8 us
    ppermute x12, starting transfers between devices, neighbours(): across = lax.ppermute(to_outer, 'gx', outer)  7.71 us
    ppermute x3, waiting for transfers between devices, relayed(): return lax.ppermute(shard, 'tm', [(i, i + 1) for i in range(length - 1)])  6.07 us
    ppermute x3, starting transfers between devices, relayed(): return lax.ppermute(shard, 'tm', [(i, i + 1) for i in range(length - 1)])  5.8 us
    ppermute x3, waiting for transfers between devices, relayed(): lax.ppermute(shard, 'tm', [(i, (i + 1) % length) for i in range(length)])  4.74 us
    pallas_call x4, Pallas kernels, products(): pl.pallas_call(body, out_shape=jax.ShapeDtypeStruct((slabs, rows, columns...  2.37 us
    ppermute x3, starting transfers between devices, relayed(): lax.ppermute(shard, 'tm', [(i, (i + 1) % length) for i in range(length)])  1.75 us
  transfers between devices with their start and end apart: 30, of which 15 were waited for; matrix products, arithmetic and copies ran while one was open for 4% of the time, Pallas kernels for 4%

commit v1 on v0

--- a/solution.py
+++ b/solution.py
@@ -11,7 +11,8 @@
 
 SWEEPS = 2
 SHARES = (9, 11, 12)
-RING = ("100", "110")
+RING = ("101", "100")
+
 
 spacing = 2.0
 step_size = 0.2
@@ -116,6 +117,34 @@
     )(*parts, *halves_y, *halves_z)
 
 
+def fetched(node_values, nodes, ends):
+    _, _, slabs, _, columns = node_values.shape
+    spans = [(m, a, b) for m in nodes for a, b in zip(ends, ends[1:])]
+
+    def body(source, *refs):
+        sems = refs[-1]
+        copies = [
+            pltpu.make_async_copy(source.at[0, m, :, pl.ds(a, b - a), :], refs[k], sems.at[k])
+            for k, (m, a, b) in enumerate(spans)
+        ]
+        for copy in copies:
+            copy.start()
+        for copy in copies:
+            copy.wait()
+
+    vmem = pl.BlockSpec(memory_space=pltpu.VMEM)
+    parts = pl.pallas_call(
+        body,
+        out_shape=[jax.ShapeDtypeStruct((slabs, b - a, columns), jnp.float32) for _, a, b in spans],
+        in_specs=[pl.BlockSpec(memory_space=pltpu.HBM)],
+        out_specs=[vmem] * len(spans),
+        scratch_shapes=[pltpu.SemaphoreType.DMA((len(spans),))],
+        compiler_params=pltpu.CompilerParams(vmem_limit_bytes=8 * 1024 * 1024),
+    )(pltpu.with_memory_space_constraint(node_values, pltpu.HBM))
+    size = len(ends) - 1
+    return [parts[i * size : (i + 1) * size] for i in range(len(nodes))]
+
+
 def weighted(weights, parts):
     return sum(w * p for w, p in zip(weights, parts))
 
@@ -130,7 +159,9 @@
     cut = lambda item: jnp.split(item, cuts, axis=1)
     join = lambda items: jnp.concatenate(items, axis=1)
     start = cut(initial)
-    values = [cut(node_values[0, m]) for m in range(3)]
+    ends = [0] + cuts + [rows]
+    (last_node,) = fetched(node_values, (2,), ends)
+    values = [*fetched(node_values, (0, 1), ends), last_node]
     for sweep in range(SWEEPS):
         old = list(zip(*values))
         linear_one = [weighted(MIDDLE, u) for u in old]

time: 68.1 us -> 67.7 us (level)
  Pallas kernels: 2.37 us -> 4.87 us
  local copies, waits for them, and re-layouts: 1.58 us -> 0.02 us
  waiting for transfers between devices: 32.7 us -> 31.2 us
    pallas_call x0 -> x2, Pallas kernels: none -> 2.51 us  [fetched(): pl.pallas_call(body, out_shape=[jax.ShapeDtypeStruct((slabs, b - a, colum...]
    ppermute x3, waiting for transfers between devices: 4.74 us -> 2.48 us  [relayed(): lax.ppermute(shard, 'tm', [(i, (i + 1) % length) for i in range(length)])]
    ppermute x3, waiting for transfers between devices: 6.07 us -> 7.67 us  [relayed(): return lax.ppermute(shard, 'tm', [(i, i + 1) for i in range(length - 1)])]
    squeeze x1 -> x0, local copies, waits for them, and re-layouts: 1.52 us -> none  [sweeps(): values = [cut(node_values[0, m]) for m in range(3)]]
    ppermute x12, waiting for transfers between devices: 21.8 us -> 21 us  [neighbours(): across = lax.ppermute(to_outer, 'gx', outer)]
  transfers between devices with their start and end apart: 30 -> 30, of which waited for: 15 -> 14; matrix products, arithmetic and copies ran while one was open for 4% -> 4% of each run, Pallas kernels for 4% -> 6%
where the time goes in v1:
time: 67.7 us; the launch traced here: 66.5 us
  waiting for transfers between devices  31.2 us (46%)
  starting transfers between devices  26.2 us (39%)
  Pallas kernels  4.87 us (7%)
  other arithmetic  3.75 us (6%)
    ppermute x12, waiting for transfers between devices, neighbours(): across = lax.ppermute(to_outer, 'gx', outer)  21 us
    ppermute x12, starting transfers between devices, neighbours(): beside = lax.ppermute(to_inner, 'gx', inner)  10.8 us
    ppermute x12, starting transfers between devices, neighbours(): across = lax.ppermute(to_outer, 'gx', outer)  7.73 us
    ppermute x3, waiting for transfers between devices, relayed(): return lax.ppermute(shard, 'tm', [(i, i + 1) for i in range(length - 1)])  7.67 us
    ppermute x3, starting transfers between devices, relayed(): return lax.ppermute(shard, 'tm', [(i, i + 1) for i in range(length - 1)])  6 us
    pallas_call x2, Pallas kernels, fetched(): pl.pallas_call(body, out_shape=[jax.ShapeDtypeStruct((slabs, b - a, colum...  2.51 us
    ppermute x3, waiting for transfers between devices, relayed(): lax.ppermute(shard, 'tm', [(i, (i + 1) % length) for i in range(length)])  2.48 us
    pallas_call x4, Pallas kernels, products(): pl.pallas_call(body, out_shape=jax.ShapeDtypeStruct((slabs, rows, columns...  2.36 us
  transfers between devices with their start and end apart: 30, of which 14 were waited for; matrix products, arithmetic and copies ran while one was open for 4% of the time, Pallas kernels for 6%

profile of v1, /device:TPU:29, one launch (start us, length us, event | category | flops | bytes accessed | tf_op | source)
XLA Modules:
  0.0 66.5 jit_solution(16735082752076742435)
XLA Ops:
  0.0 1.2 %shard_map.64 = (f32[2,72,256]{2,1,0:T(8,128)S(1)}, f32[2,88,256]{2,1,0:T(8,128)S(1)}, f32[2,96,256]{2,1,0:T(8,128)S(1)}) custom-call(f32[1,3,2,256,256]{4,3,2,1,0:T(8,128)} %source.3), custom_call_target="tpu_custom_call" | custom-call | tf_op jit(solution)/shard_map/pallas_call | solution.py:136
  1.2 1.3 %collective-permute-start = (f32[2,72,256]{2,1,0:T(8,128)S(1)}, f32[2,72,256]{2,1,0:T(8,128)S(1)}, u32[]{:S(2)}, u32[]{:S(2)}) collective-permute-start(f32[2,72,256]{2,1,0:T(8,128)S(1)} %get-tuple-element.14), channel_id=1, source_target_pairs={{0,4},{4,8},{8,12},{12,16},{16,20},{20,24},{24,28},{28,0},{1,5},{5... | collective-permute-start | bytes 442376 | tf_op jit(solution)/shard_map/ppermute | solution.py:46
  2.4 1.9 %collective-permute-start.1 = (f32[2,88,256]{2,1,0:T(8,128)S(1)}, f32[2,88,256]{2,1,0:T(8,128)S(1)}, u32[]{:S(2)}, u32[]{:S(2)}) collective-permute-start(f32[2,88,256]{2,1,0:T(8,128)S(1)} %get-tuple-element.17), channel_id=1, source_target_pairs={{0,4},{4,8},{8,12},{12,16},{16,20},{20,24},{24,28},{1,5},{5,9},{9,... | collective-permute-start | bytes 540680 | tf_op jit(solution)/shard_map/ppermute | solution.py:47
  4.4 1.3 %shard_map.65 = (f32[2,72,256]{2,1,0:T(8,128)S(1)}, f32[2,88,256]{2,1,0:T(8,128)S(1)}, f32[2,96,256]{2,1,0:T(8,128)S(1)}, f32[2,72,256]{2,1,0:T(8,128)S(1)}, f32...) custom-call(f32[1,3,2,256,256]{4,3,2,1,0:T(8,128)} %source.3), custom_call_target="tpu_custom_call" | custom-call | tf_op jit(solution)/shard_map/pallas_call | solution.py:136
  7.0 1.7 %collective-permute-start.4 = (f32[2,72,256]{2,1,0:T(8,128)S(1)}, f32[2,72,256]{2,1,0:T(8,128)S(1)}, u32[]{:S(2)}, u32[]{:S(2)}) collective-permute-start(f32[2,72,256]{2,1,0:T(8,128)S(1)} %get-tuple-element.45.refs_0_), channel_id=1, source_target_pairs={{0,1},{1,0},{2,3},{3,2},{4,5},{5,4},{6,7},{7,6},{8,9},{9,8},{10,11... | collective-permute-start | bytes 442376 | tf_op jit(solution)/shard_map/ppermute | solution.py:68
  8.8 1.7 %collective-permute-done.1 = f32[2,88,256]{2,1,0:T(8,128)S(1)} collective-permute-done((f32[2,88,256]{2,1,0:T(8,128)S(1)}, f32[2,88,256]{2,1,0:T(8,128)S(1)}, u32[]{:S(2)}, u32[]{:S(2)}) %collective-permute-start.1) | collective-permute-done | bytes 180256 | tf_op jit(solution)/shard_map/ppermute | solution.py:47
  10.6 3.2 %collective-permute-start.6 = (f32[2,88,256]{2,1,0:T(8,128)S(1)}, f32[2,88,256]{2,1,0:T(8,128)S(1)}, u32[]{:S(2)}, u32[]{:S(2)}) collective-permute-start(f32[2,88,256]{2,1,0:T(8,128)S(1)} %get-tuple-element.43.refs_1_), channel_id=1, source_target_pairs={{0,1},{1,0},{2,3},{3,2},{4,5},{5,4},{6,7},{7,6},{8,9},{9,8},{10,11... | collective-permute-start | bytes 540680 | tf_op jit(solution)/shard_map/ppermute | solution.py:68
  14.8 1.8 %collective-permute-start.8 = (f32[2,96,256]{2,1,0:T(8,128)S(1)}, f32[2,96,256]{2,1,0:T(8,128)S(1)}, u32[]{:S(2)}, u32[]{:S(2)}) collective-permute-start(f32[2,96,256]{2,1,0:T(8,128)S(1)} %get-tuple-element.41.refs_2_), channel_id=1, source_target_pairs={{0,1},{1,0},{2,3},{3,2},{4,5},{5,4},{6,7},{7,6},{8,9},{9,8},{10,11... | collective-permute-start | bytes 589832 | tf_op jit(solution)/shard_map/ppermute | solution.py:68
  18.2 1.2 %collective-permute-start.9 = (f32[2,72,256]{2,1,0:T(8,128)S(1)}, f32[2,72,256]{2,1,0:T(8,128)S(1)}, u32[]{:S(2)}, u32[]{:S(2)}) collective-permute-start(f32[2,72,256]{2,1,0:T(8,128)S(1)} %get-tuple-element.39.refs_0_), channel_id=1, source_target_pairs={{1,2},{2,1},{3,0},{0,3},{5,6},{6,5},{7,4},{4,7},{9,10},{10,9},{11,... | collective-permute-start | bytes 442376 | tf_op jit(solution)/shard_map/ppermute | solution.py:67
  19.4 1.2 %collective-permute-done.5 = f32[2,88,256]{2,1,0:T(8,128)S(1)} collective-permute-done((f32[2,88,256]{2,1,0:T(8,128)S(1)}, f32[2,88,256]{2,1,0:T(8,128)S(1)}, u32[]{:S(2)}, u32[]{:S(2)}) %collective-permute-start.5) | collective-permute-done | bytes 180256 | tf_op jit(solution)/shard_map/ppermute | solution.py:67
  21.6 3.3 %collective-permute-done.7 = f32[2,96,256]{2,1,0:T(8,128)S(1)} collective-permute-done((f32[2,96,256]{2,1,0:T(8,128)S(1)}, f32[2,96,256]{2,1,0:T(8,128)S(1)}, u32[]{:S(2)}, u32[]{:S(2)}) %collective-permute-start.7) | collective-permute-done | bytes 196640 | tf_op jit(solution)/shard_map/ppermute | solution.py:67
  26.5 1.5 %collective-permute-done.9 = f32[2,72,256]{2,1,0:T(8,128)S(1)} collective-permute-done((f32[2,72,256]{2,1,0:T(8,128)S(1)}, f32[2,72,256]{2,1,0:T(8,128)S(1)}, u32[]{:S(2)}, u32[]{:S(2)}) %collective-permute-start.9) | collective-permute-done | bytes 147488 | tf_op jit(solution)/shard_map/ppermute | solution.py:67
  28.5 3.4 %collective-permute-done.12 = f32[2,88,256]{2,1,0:T(8,128)S(1)} collective-permute-done((f32[2,88,256]{2,1,0:T(8,128)S(1)}, f32[2,88,256]{2,1,0:T(8,128)S(1)}, u32[]{:S(2)}, u32[]{:S(2)}) %collective-permute-start.12) | collective-permute-done | bytes 180256 | tf_op jit(solution)/shard_map/ppermute | solution.py:67
  32.1 2.2 %collective-permute-start.14 = (f32[2,88,256]{2,1,0:T(8,128)S(1)}, f32[2,88,256]{2,1,0:T(8,128)S(1)}, u32[]{:S(2)}, u32[]{:S(2)}) collective-permute-start(f32[2,88,256]{2,1,0:T(8,128)S(1)} %fusion.13), channel_id=1, source_target_pairs={{0,4},{4,8},{8,12},{12,16},{16,20},{20,24},{24,28},{1,5},{5,9},{9,... | collective-permute-start | bytes 540680 | tf_op jit(solution)/shard_map/ppermute | solution.py:47
  35.9 1.9 %collective-permute-start.17 = (f32[2,96,256]{2,1,0:T(8,128)S(1)}, f32[2,96,256]{2,1,0:T(8,128)S(1)}, u32[]{:S(2)}, u32[]{:S(2)}) collective-permute-start(f32[2,96,256]{2,1,0:T(8,128)S(1)} %fusion.3), channel_id=1, source_target_pairs={{0,4},{4,8},{8,12},{12,16},{16,20},{20,24},{24,28},{1,5},{5,9},{9,... | collective-permute-start | bytes 589832 | tf_op jit(solution)/shard_map/ppermute | solution.py:47
  37.9 3.4 %collective-permute-done.14 = f32[2,88,256]{2,1,0:T(8,128)S(1)} collective-permute-done((f32[2,88,256]{2,1,0:T(8,128)S(1)}, f32[2,88,256]{2,1,0:T(8,128)S(1)}, u32[]{:S(2)}, u32[]{:S(2)}) %collective-permute-start.14) | collective-permute-done | bytes 180256 | tf_op jit(solution)/shard_map/ppermute | solution.py:47
  42.2 2.5 %collective-permute-done.17 = f32[2,96,256]{2,1,0:T(8,128)S(1)} collective-permute-done((f32[2,96,256]{2,1,0:T(8,128)S(1)}, f32[2,96,256]{2,1,0:T(8,128)S(1)}, u32[]{:S(2)}, u32[]{:S(2)}) %collective-permute-start.17) | collective-permute-done | bytes 196640 | tf_op jit(solution)/shard_map/ppermute | solution.py:47
  45.6 1.4 %collective-permute-start.25 = (f32[2,72,256]{2,1,0:T(8,128)S(1)}, f32[2,72,256]{2,1,0:T(8,128)S(1)}, u32[]{:S(2)}, u32[]{:S(2)}) collective-permute-start(f32[2,72,256]{2,1,0:T(8,128)S(1)} %get-tuple-element.27.refs_0_), channel_id=1, source_target_pairs={{0,1},{1,0},{2,3},{3,2},{4,5},{5,4},{6,7},{7,6},{8,9},{9,8},{10,11... | collective-permute-start | bytes 442376 | tf_op jit(solution)/shard_map/ppermute | solution.py:68
  46.9 1.2 %collective-permute-start.24 = (f32[2,72,256]{2,1,0:T(8,128)S(1)}, f32[2,72,256]{2,1,0:T(8,128)S(1)}, u32[]{:S(2)}, u32[]{:S(2)}) collective-permute-start(f32[2,72,256]{2,1,0:T(8,128)S(1)} %get-tuple-element.27.refs_0_), channel_id=1, source_target_pairs={{1,2},{2,1},{3,0},{0,3},{5,6},{6,5},{7,4},{4,7},{9,10},{10,9},{11,... | collective-permute-start | bytes 442376 | tf_op jit(solution)/shard_map/ppermute | solution.py:67
  49.6 1.2 %collective-permute-start.26 = (f32[2,88,256]{2,1,0:T(8,128)S(1)}, f32[2,88,256]{2,1,0:T(8,128)S(1)}, u32[]{:S(2)}, u32[]{:S(2)}) collective-permute-start(f32[2,88,256]{2,1,0:T(8,128)S(1)} %get-tuple-element.25.refs_1_), channel_id=1, source_target_pairs={{1,2},{2,1},{3,0},{0,3},{5,6},{6,5},{7,4},{4,7},{9,10},{10,9},{11,... | collective-permute-start | bytes 540680 | tf_op jit(solution)/shard_map/ppermute | solution.py:67
  50.8 2.5 %collective-permute-done.24 = f32[2,72,256]{2,1,0:T(8,128)S(1)} collective-permute-done((f32[2,72,256]{2,1,0:T(8,128)S(1)}, f32[2,72,256]{2,1,0:T(8,128)S(1)}, u32[]{:S(2)}, u32[]{:S(2)}) %collective-permute-start.24) | collective-permute-done | bytes 147488 | tf_op jit(solution)/shard_map/ppermute | solution.py:67
  53.5 4.1 %collective-permute-done.22 = f32[2,96,256]{2,1,0:T(8,128)S(1)} collective-permute-done((f32[2,96,256]{2,1,0:T(8,128)S(1)}, f32[2,96,256]{2,1,0:T(8,128)S(1)}, u32[]{:S(2)}, u32[]{:S(2)}) %collective-permute-start.22) | collective-permute-done | bytes 196640 | tf_op jit(solution)/shard_map/ppermute | solution.py:67
  58.5 1.6 %collective-permute-start.28 = (f32[2,96,256]{2,1,0:T(8,128)S(1)}, f32[2,96,256]{2,1,0:T(8,128)S(1)}, u32[]{:S(2)}, u32[]{:S(2)}) collective-permute-start(f32[2,96,256]{2,1,0:T(8,128)S(1)} %get-tuple-element.23.refs_2_), channel_id=1, source_target_pairs={{1,2},{2,1},{3,0},{0,3},{5,6},{6,5},{7,4},{4,7},{9,10},{10,9},{11,... | collective-permute-start | bytes 589832 | tf_op jit(solution)/shard_map/ppermute | solution.py:67
  60.8 4.8 %collective-permute-done.28 = f32[2,96,256]{2,1,0:T(8,128)S(1)} collective-permute-done((f32[2,96,256]{2,1,0:T(8,128)S(1)}, f32[2,96,256]{2,1,0:T(8,128)S(1)}, u32[]{:S(2)}, u32[]{:S(2)}) %collective-permute-start.28) | collective-permute-done | bytes 196640 | tf_op jit(solution)/shard_map/ppermute | solution.py:67
  (95 shorter events, 14.4 us)
Async XLA Ops:
  2.4 8.1 %collective-permute-start.1 = (f32[2,88,256]{2,1,0:T(8,128)S(1)}, f32[2,88,256]{2,1,0:T(8,128)S(1)}, u32[]{:S(2)}, u32[]{:S(2)}) collective-permute-start(f32[2,88,256]{2,1,0:T(8,128)S(1)} %get-tuple-element.17), channel_id=1, source_target_pairs={{0,4},{4,8},{8,12},{12,16},{16,20},{20,24},{24,28},{1,5},{5,9},{9,... | collective-permute-start | bytes 540680 | tf_op jit(solution)/shard_map/ppermute | solution.py:47
  4.4 10.4 %collective-permute-start.2 = (f32[2,96,256]{2,1,0:T(8,128)S(1)}, f32[2,96,256]{2,1,0:T(8,128)S(1)}, u32[]{:S(2)}, u32[]{:S(2)}) collective-permute-start(f32[2,96,256]{2,1,0:T(8,128)S(1)} %get-tuple-element.20), channel_id=1, source_target_pairs={{0,4},{4,8},{8,12},{12,16},{16,20},{20,24},{24,28},{28,0},{1,5},{5... | collective-permute-start | bytes 589832 | tf_op jit(solution)/shard_map/ppermute | solution.py:46
  7.0 10.3 %collective-permute-start.4 = (f32[2,72,256]{2,1,0:T(8,128)S(1)}, f32[2,72,256]{2,1,0:T(8,128)S(1)}, u32[]{:S(2)}, u32[]{:S(2)}) collective-permute-start(f32[2,72,256]{2,1,0:T(8,128)S(1)} %get-tuple-element.45.refs_0_), channel_id=1, source_target_pairs={{0,1},{1,0},{2,3},{3,2},{4,5},{5,4},{6,7},{7,6},{8,9},{9,8},{10,11... | collective-permute-start | bytes 442376 | tf_op jit(solution)/shard_map/ppermute | solution.py:68
  8.6 8.8 %collective-permute-start.3 = (f32[2,72,256]{2,1,0:T(8,128)S(1)}, f32[2,72,256]{2,1,0:T(8,128)S(1)}, u32[]{:S(2)}, u32[]{:S(2)}) collective-permute-start(f32[2,72,256]{2,1,0:T(8,128)S(1)} %get-tuple-element.45.refs_0_), channel_id=1, source_target_pairs={{1,2},{2,1},{3,0},{0,3},{5,6},{6,5},{7,4},{4,7},{9,10},{10,9},{11,... | collective-permute-start | bytes 442376 | tf_op jit(solution)/shard_map/ppermute | solution.py:67
  10.6 7.6 %collective-permute-start.6 = (f32[2,88,256]{2,1,0:T(8,128)S(1)}, f32[2,88,256]{2,1,0:T(8,128)S(1)}, u32[]{:S(2)}, u32[]{:S(2)}) collective-permute-start(f32[2,88,256]{2,1,0:T(8,128)S(1)} %get-tuple-element.43.refs_1_), channel_id=1, source_target_pairs={{0,1},{1,0},{2,3},{3,2},{4,5},{5,4},{6,7},{7,6},{8,9},{9,8},{10,11... | collective-permute-start | bytes 540680 | tf_op jit(solution)/shard_map/ppermute | solution.py:68
  13.7 6.9 %collective-permute-start.5 = (f32[2,88,256]{2,1,0:T(8,128)S(1)}, f32[2,88,256]{2,1,0:T(8,128)S(1)}, u32[]{:S(2)}, u32[]{:S(2)}) collective-permute-start(f32[2,88,256]{2,1,0:T(8,128)S(1)} %get-tuple-element.43.refs_1_), channel_id=1, source_target_pairs={{1,2},{2,1},{3,0},{0,3},{5,6},{6,5},{7,4},{4,7},{9,10},{10,9},{11,... | collective-permute-start | bytes 540680 | tf_op jit(solution)/shard_map/ppermute | solution.py:67
  17.2 7.6 %collective-permute-start.7 = (f32[2,96,256]{2,1,0:T(8,128)S(1)}, f32[2,96,256]{2,1,0:T(8,128)S(1)}, u32[]{:S(2)}, u32[]{:S(2)}) collective-permute-start(f32[2,96,256]{2,1,0:T(8,128)S(1)} %get-tuple-element.41.refs_2_), channel_id=1, source_target_pairs={{1,2},{2,1},{3,0},{0,3},{5,6},{6,5},{7,4},{4,7},{9,10},{10,9},{11,... | collective-permute-start | bytes 589832 | tf_op jit(solution)/shard_map/ppermute | solution.py:67
  17.6 8.1 %collective-permute-start.10 = (f32[2,72,256]{2,1,0:T(8,128)S(1)}, f32[2,72,256]{2,1,0:T(8,128)S(1)}, u32[]{:S(2)}, u32[]{:S(2)}) collective-permute-start(f32[2,72,256]{2,1,0:T(8,128)S(1)} %get-tuple-element.39.refs_0_), channel_id=1, source_target_pairs={{0,1},{1,0},{2,3},{3,2},{4,5},{5,4},{6,7},{7,6},{8,9},{9,8},{10,11... | collective-permute-start | bytes 442376 | tf_op jit(solution)/shard_map/ppermute | solution.py:68
  18.2 9.8 %collective-permute-start.9 = (f32[2,72,256]{2,1,0:T(8,128)S(1)}, f32[2,72,256]{2,1,0:T(8,128)S(1)}, u32[]{:S(2)}, u32[]{:S(2)}) collective-permute-start(f32[2,72,256]{2,1,0:T(8,128)S(1)} %get-tuple-element.39.refs_0_), channel_id=1, source_target_pairs={{1,2},{2,1},{3,0},{0,3},{5,6},{6,5},{7,4},{4,7},{9,10},{10,9},{11,... | collective-permute-start | bytes 442376 | tf_op jit(solution)/shard_map/ppermute | solution.py:67
  20.9 7.6 %collective-permute-start.13 = (f32[2,88,256]{2,1,0:T(8,128)S(1)}, f32[2,88,256]{2,1,0:T(8,128)S(1)}, u32[]{:S(2)}, u32[]{:S(2)}) collective-permute-start(f32[2,88,256]{2,1,0:T(8,128)S(1)} %get-tuple-element.37.refs_1_), channel_id=1, source_target_pairs={{0,1},{1,0},{2,3},{3,2},{4,5},{5,4},{6,7},{7,6},{8,9},{9,8},{10,11... | collective-permute-start | bytes 540680 | tf_op jit(solution)/shard_map/ppermute | solution.py:68
  21.0 10.9 %collective-permute-start.12 = (f32[2,88,256]{2,1,0:T(8,128)S(1)}, f32[2,88,256]{2,1,0:T(8,128)S(1)}, u32[]{:S(2)}, u32[]{:S(2)}) collective-permute-start(f32[2,88,256]{2,1,0:T(8,128)S(1)} %get-tuple-element.37.refs_1_), channel_id=1, source_target_pairs={{1,2},{2,1},{3,0},{0,3},{5,6},{6,5},{7,4},{4,7},{9,10},{10,9},{11,... | collective-permute-start | bytes 540680 | tf_op jit(solution)/shard_map/ppermute | solution.py:67
  25.1 10.6 %collective-permute-start.16 = (f32[2,96,256]{2,1,0:T(8,128)S(1)}, f32[2,96,256]{2,1,0:T(8,128)S(1)}, u32[]{:S(2)}, u32[]{:S(2)}) collective-permute-start(f32[2,96,256]{2,1,0:T(8,128)S(1)} %get-tuple-element.35.refs_2_), channel_id=1, source_target_pairs={{0,1},{1,0},{2,3},{3,2},{4,5},{5,4},{6,7},{7,6},{8,9},{9,8},{10,11... | collective-permute-start | bytes 589832 | tf_op jit(solution)/shard_map/ppermute | solution.py:68
  25.8 9.9 %collective-permute-start.15 = (f32[2,96,256]{2,1,0:T(8,128)S(1)}, f32[2,96,256]{2,1,0:T(8,128)S(1)}, u32[]{:S(2)}, u32[]{:S(2)}) collective-permute-start(f32[2,96,256]{2,1,0:T(8,128)S(1)} %get-tuple-element.35.refs_2_), channel_id=1, source_target_pairs={{1,2},{2,1},{3,0},{0,3},{5,6},{6,5},{7,4},{4,7},{9,10},{10,9},{11,... | collective-permute-start | bytes 589832 | tf_op jit(solution)/shard_map/ppermute | solution.py:67
  28.2 6.7 %collective-permute-start.11 = (f32[2,72,256]{2,1,0:T(8,128)S(1)}, f32[2,72,256]{2,1,0:T(8,128)S(1)}, u32[]{:S(2)}, u32[]{:S(2)}) collective-permute-start(f32[2,72,256]{2,1,0:T(8,128)S(1)} %fusion.23), channel_id=1, source_target_pairs={{0,4},{4,8},{8,12},{12,16},{16,20},{20,24},{24,28},{28,0},{1,5},{5... | collective-permute-start | bytes 442376 | tf_op jit(solution)/shard_map/ppermute | solution.py:46
  32.1 9.2 %collective-permute-start.14 = (f32[2,88,256]{2,1,0:T(8,128)S(1)}, f32[2,88,256]{2,1,0:T(8,128)S(1)}, u32[]{:S(2)}, u32[]{:S(2)}) collective-permute-start(f32[2,88,256]{2,1,0:T(8,128)S(1)} %fusion.13), channel_id=1, source_target_pairs={{0,4},{4,8},{8,12},{12,16},{16,20},{20,24},{24,28},{1,5},{5,9},{9,... | collective-permute-start | bytes 540680 | tf_op jit(solution)/shard_map/ppermute | solution.py:47
  34.9 7.2 %collective-permute-start.19 = (f32[2,72,256]{2,1,0:T(8,128)S(1)}, f32[2,72,256]{2,1,0:T(8,128)S(1)}, u32[]{:S(2)}, u32[]{:S(2)}) collective-permute-start(f32[2,72,256]{2,1,0:T(8,128)S(1)} %get-tuple-element.33.refs_0_), channel_id=1, source_target_pairs={{0,1},{1,0},{2,3},{3,2},{4,5},{5,4},{6,7},{7,6},{8,9},{9,8},{10,11... | collective-permute-start | bytes 442376 | tf_op jit(solution)/shard_map/ppermute | solution.py:68
  35.5 6.6 %collective-permute-start.18 = (f32[2,72,256]{2,1,0:T(8,128)S(1)}, f32[2,72,256]{2,1,0:T(8,128)S(1)}, u32[]{:S(2)}, u32[]{:S(2)}) collective-permute-start(f32[2,72,256]{2,1,0:T(8,128)S(1)} %get-tuple-element.33.refs_0_), channel_id=1, source_target_pairs={{1,2},{2,1},{3,0},{0,3},{5,6},{6,5},{7,4},{4,7},{9,10},{10,9},{11,... | collective-permute-start | bytes 442376 | tf_op jit(solution)/shard_map/ppermute | solution.py:67
  35.9 8.8 %collective-permute-start.17 = (f32[2,96,256]{2,1,0:T(8,128)S(1)}, f32[2,96,256]{2,1,0:T(8,128)S(1)}, u32[]{:S(2)}, u32[]{:S(2)}) collective-permute-start(f32[2,96,256]{2,1,0:T(8,128)S(1)} %fusion.3), channel_id=1, source_target_pairs={{0,4},{4,8},{8,12},{12,16},{16,20},{20,24},{24,28},{1,5},{5,9},{9,... | collective-permute-start | bytes 589832 | tf_op jit(solution)/shard_map/ppermute | solution.py:47
  41.4 7.2 %collective-permute-start.21 = (f32[2,88,256]{2,1,0:T(8,128)S(1)}, f32[2,88,256]{2,1,0:T(8,128)S(1)}, u32[]{:S(2)}, u32[]{:S(2)}) collective-permute-start(f32[2,88,256]{2,1,0:T(8,128)S(1)} %get-tuple-element.31.refs_1_), channel_id=1, source_target_pairs={{0,1},{1,0},{2,3},{3,2},{4,5},{5,4},{6,7},{7,6},{8,9},{9,8},{10,11... | collective-permute-start | bytes 540680 | tf_op jit(solution)/shard_map/ppermute | solution.py:68
  42.0 6.9 %collective-permute-start.20 = (f32[2,88,256]{2,1,0:T(8,128)S(1)}, f32[2,88,256]{2,1,0:T(8,128)S(1)}, u32[]{:S(2)}, u32[]{:S(2)}) collective-permute-start(f32[2,88,256]{2,1,0:T(8,128)S(1)} %get-tuple-element.31.refs_1_), channel_id=1, source_target_pairs={{1,2},{2,1},{3,0},{0,3},{5,6},{6,5},{7,4},{4,7},{9,10},{10,9},{11,... | collective-permute-start | bytes 540680 | tf_op jit(solution)/shard_map/ppermute | solution.py:67
  48.6 9.0 %collective-permute-start.22 = (f32[2,96,256]{2,1,0:T(8,128)S(1)}, f32[2,96,256]{2,1,0:T(8,128)S(1)}, u32[]{:S(2)}, u32[]{:S(2)}) collective-permute-start(f32[2,96,256]{2,1,0:T(8,128)S(1)} %get-tuple-element.29.refs_2_), channel_id=1, source_target_pairs={{1,2},{2,1},{3,0},{0,3},{5,6},{6,5},{7,4},{4,7},{9,10},{10,9},{11,... | collective-permute-start | bytes 589832 | tf_op jit(solution)/shard_map/ppermute | solution.py:67
  49.1 11.3 %collective-permute-start.27 = (f32[2,88,256]{2,1,0:T(8,128)S(1)}, f32[2,88,256]{2,1,0:T(8,128)S(1)}, u32[]{:S(2)}, u32[]{:S(2)}) collective-permute-start(f32[2,88,256]{2,1,0:T(8,128)S(1)} %get-tuple-element.25.refs_1_), channel_id=1, source_target_pairs={{0,1},{1,0},{2,3},{3,2},{4,5},{5,4},{6,7},{7,6},{8,9},{9,8},{10,11... | collective-permute-start | bytes 540680 | tf_op jit(solution)/shard_map/ppermute | solution.py:68
  49.6 10.9 %collective-permute-start.26 = (f32[2,88,256]{2,1,0:T(8,128)S(1)}, f32[2,88,256]{2,1,0:T(8,128)S(1)}, u32[]{:S(2)}, u32[]{:S(2)}) collective-permute-start(f32[2,88,256]{2,1,0:T(8,128)S(1)} %get-tuple-element.25.refs_1_), channel_id=1, source_target_pairs={{1,2},{2,1},{3,0},{0,3},{5,6},{6,5},{7,4},{4,7},{9,10},{10,9},{11,... | collective-permute-start | bytes 540680 | tf_op jit(solution)/shard_map/ppermute | solution.py:67
  58.5 7.0 %collective-permute-start.28 = (f32[2,96,256]{2,1,0:T(8,128)S(1)}, f32[2,96,256]{2,1,0:T(8,128)S(1)}, u32[]{:S(2)}, u32[]{:S(2)}) collective-permute-start(f32[2,96,256]{2,1,0:T(8,128)S(1)} %get-tuple-element.23.refs_2_), channel_id=1, source_target_pairs={{1,2},{2,1},{3,0},{0,3},{5,6},{6,5},{7,4},{4,7},{9,10},{10,9},{11,... | collective-permute-start | bytes 589832 | tf_op jit(solution)/shard_map/ppermute | solution.py:67
  (10 other events, 61.1 us)
